TPU v7x, 32 devices: a whole 2x2x4 slice. The times are simulated.
32 devices in a mesh: shot: 4 (over z), gx: 4 (over x, core), gy: 2 (over y).
Axes of the slice: x: 2, y: 2, z: 4, core: 2. Of those that a mesh axis runs over, the one named last changes fastest.
Arguments:
- partials: float32 [4, 9, 4, 32, 256], P('shot', None, None, 'gx', 'gy'), may hold values from -16 to 16, as said below
- hist_s: float32 [5, 3, 4, 32, 256], P(None, None, 'shot', 'gx', 'gy'), may hold values from -30 to 30
- hist_y: float32 [5, 3, 4, 32, 256], P(None, None, 'shot', 'gx', 'gy'), may hold values from -70 to 70, as said below
Outputs:
- direction: float32 [3, 4, 32, 256], P(None, 'shot', 'gx', 'gy')
Inputs may be any that keep to these rules, and one draw needn't show every extreme that they name: `partials`: for every shot group and cell, entries 3, 4, 5 are positive and each exceeds the sum of the magnitudes of the two off-diagonal entries of its row of the 3x3 matrix [[e3, e6, e7], [e6, e4, e8], [e7, e8, e5]]. Each entry of hist_y times the matching entry of hist_s is at least 0.2 times the square of that hist_s entry.
All inputs are finite; a program needn't handle non-finite values.
Results may differ from a plain program's by a relative error of at most 0.00013.
Values sent between devices are 32-bit elements; how exact they have to be, the bound alone decides.
No kernel may reach another device: no remote copies, remote signals or barrier semaphores. Data moves between devices by JAX's collectives and lax.ppermute only.
A program may use at most 64 MiB of HBM per device.

v0:
```python
import jax
import jax.numpy as jnp
from jax import lax
from jax.sharding import PartitionSpec as P

PAIRS = 5


def extended_2(cells, sides, width):
    for axis, dim in sides:
        count = lax.axis_size(axis)
        ends = count - 1
        head = lax.slice_in_dim(cells, 0, width, axis=dim)
        tail = lax.slice_in_dim(cells, cells.shape[dim] - width, cells.shape[dim], axis=dim)
        cells = jnp.concatenate(
            [
                lax.ppermute(tail, axis, [(i, (i + 1) % count) for i in range(ends)]),
                cells,
                lax.ppermute(head, axis, [((i + 1) % count, i) for i in range(ends)]),
            ],
            axis=dim,
        )
    return cells


def smooth_block(padded):
    along_x = 0.25 * (padded[:, :, :-2] + 2.0 * padded[:, :, 1:-1] + padded[:, :, 2:])
    return 0.25 * (along_x[..., :-2] + 2.0 * along_x[..., 1:-1] + along_x[..., 2:])


def apply_inverse(hessian, vectors):
    diag_p = hessian[0]
    diag_s = hessian[1]
    diag_r = hessian[2]
    cross_ps = hessian[3]
    cross_pr = hessian[4]
    cross_sr = hessian[5]
    cof_pp = diag_s * diag_r - cross_sr * cross_sr
    cof_ps = cross_pr * cross_sr - cross_ps * diag_r
    cof_pr = cross_ps * cross_sr - diag_s * cross_pr
    cof_ss = diag_p * diag_r - cross_pr * cross_pr
    cof_sr = cross_ps * cross_pr - diag_p * cross_sr
    cof_rr = diag_p * diag_s - cross_ps * cross_ps
    determinant = diag_p * cof_pp + cross_ps * cof_ps + cross_pr * cof_pr
    inverse_det = 1.0 / determinant
    comp_one = vectors[:, 0]
    comp_two = vectors[:, 1]
    comp_three = vectors[:, 2]
    return jnp.stack(
        [
            (cof_pp * comp_one + cof_ps * comp_two + cof_pr * comp_three) * inverse_det,
            (cof_ps * comp_one + cof_ss * comp_two + cof_sr * comp_three) * inverse_det,
            (cof_pr * comp_one + cof_sr * comp_two + cof_rr * comp_three) * inverse_det,
        ],
        axis=1,
    )


def pair_dots(left_flat, right_flat):
    return lax.dot_general(
        left_flat,
        right_flat,
        (((1,), (1,)), ((), ())),
        precision=lax.Precision.HIGHEST,
        preferred_element_type=jnp.float32,
    )


def upper_solve(matrix, values):
    count = matrix.shape[0]
    found = [None] * count
    for row in range(count - 1, -1, -1):
        total = values[row]
        for col in range(row + 1, count):
            total = total - matrix[row, col] * found[col]
        found[row] = total / matrix[row, row]
    return jnp.stack(found)


def upper_transpose_solve(matrix, values):
    count = matrix.shape[0]
    found = [None] * count
    for row in range(count):
        total = values[row]
        for col in range(row):
            total = total - matrix[col, row] * found[col]
        found[row] = total / matrix[row, row]
    return jnp.stack(found)


def combine_terms(cross_gram, curv_gram, hist_dot, pre_dot, solved, hist_s):
    middle_part = jnp.diag(jnp.diag(cross_gram)) + curv_gram
    coef_p = upper_solve(cross_gram, hist_dot)
    right_hand = jnp.dot(middle_part, coef_p, precision=lax.Precision.HIGHEST) - pre_dot
    coef_q = upper_transpose_solve(cross_gram, right_hand)
    update_s = jnp.tensordot(coef_q, hist_s, axes=1, precision=lax.Precision.HIGHEST)
    update_z = jnp.tensordot(coef_p, solved[1:], axes=1, precision=lax.Precision.HIGHEST)
    return -(solved[0] + update_s - update_z)


def per_device(partials, hist_s, hist_y):
    s_flat = hist_s.reshape(PAIRS, -1)
    y_flat = hist_y.reshape(PAIRS, -1)
    inverse_count = 1.0 / lax.axis_size("shot")
    level_sums = lax.psum_scatter(partials[0], "shot", scatter_dimension=1, tiled=True)
    fields = level_sums * inverse_count
    extended = extended_2(fields, (("gx", 2), ("gy", 3)), 1)
    smoothed = smooth_block(extended)
    gradient = smoothed[0:3]
    solved = apply_inverse(smoothed[3:9], jnp.concatenate([gradient[None], hist_y], axis=0))
    z_flat = solved[1:].reshape(PAIRS, -1)
    curv_part = pair_dots(y_flat, z_flat)
    hist_part = pair_dots(s_flat, gradient.reshape(1, -1))[:, 0]
    pre_part = pair_dots(y_flat, solved[0].reshape(1, -1))[:, 0]
    cross_gram, curv_gram, hist_dot, pre_dot = lax.psum(
        (pair_dots(s_flat, y_flat), curv_part, hist_part, pre_part), ("shot", "gx", "gy")
    )
    return combine_terms(cross_gram, curv_gram, hist_dot, pre_dot, solved, hist_s)


def solution(mesh):
    return jax.shard_map(
        per_device,
        mesh=mesh,
        in_specs=(
            P("shot", None, None, "gx", "gy"),
            P(None, None, "shot", "gx", "gy"),
            P(None, None, "shot", "gx", "gy"),
        ),
        out_specs=P(None, "shot", "gx", "gy"),
        check_vma=False,
    )
```

profile of v0, /device:TPU:14, one launch (start us, length us, event | category | flops | bytes accessed | tf_op | source)
XLA Modules:
  0.0 124.9 jit_solution(4067416101223130220)
XLA Ops:
  6.5 0.0 reduce-scatter.4.cloned.1.call-start
  6.5 1.6 %copy.40 = f32[1,9,4,8,128]{4,3,1,2,0:T(8,128)} copy(f32[1,9,4,8,128]{4,3,2,1,0:T(8,128)} %param.3) | data formatting | bytes 294912 | tf_op args[0]
  8.1 0.0 reduce-scatter.4.cloned.1.call-update
  8.1 19.2 %reduce-scatter.4.cloned.1.call-done = f32[9,1,8,128]{3,2,0,1:T(8,128)} async-done(((f32[9,4,8,128]{3,2,0,1:T(8,128)}), f32[9,1,8,128]{3,2,0,1:T(8,128)}) %reduce-scatter.4.cloned.1.call-update) | async-done | bytes 36880
  27.4 0.8 broadcast_multiply_fusion
  28.2 1.9 %collective-permute-start = (f32[9,1,1,128]{3,2,0,1:T(1,128)S(1)}, f32[9,1,1,128]{3,2,0,1:T(1,128)S(1)}, u32[]{:S(2)}, u32[]{:S(2)}) collective-permute-start(f32[9,1,1,128]{3,2,0,1:T(1,128)S(1)} %get-tuple-element.25), channel_id=1, source_target_pairs={{0,2},{2,4},{4,6},{1,3},{3,5},{5,7},{8,10},{10,12},{12,14},{9,11},... | collective-permute-start | bytes 13832 | tf_op jit(solution)/shard_map/ppermute | solution.py:17
  30.1 3.6 %collective-permute-start.1 = (f32[9,1,1,128]{3,2,0,1:T(1,128)S(1)}, f32[9,1,1,128]{3,2,0,1:T(1,128)S(1)}, u32[]{:S(2)}, u32[]{:S(2)}) collective-permute-start(f32[9,1,1,128]{3,2,0,1:T(1,128)S(1)} %get-tuple-element.26), channel_id=1, source_target_pairs={{2,0},{4,2},{6,4},{3,1},{5,3},{7,5},{10,8},{12,10},{14,12},{11,9},... | collective-permute-start | bytes 13832 | tf_op jit(solution)/shard_map/ppermute | solution.py:19
  33.7 0.0 collective-permute-done
  33.8 1.3 %collective-permute-done.1 = f32[9,1,1,128]{3,2,0,1:T(1,128)S(1)} collective-permute-done((f32[9,1,1,128]{3,2,0,1:T(1,128)S(1)}, f32[9,1,1,128]{3,2,0,1:T(1,128)S(1)}, u32[]{:S(2)}, u32[]{:S(2)}) %collective-permute-start.1) | collective-permute-done | bytes 4640 | tf_op jit(solution)/shard_map/ppermute | solution.py:19
  35.1 0.0 copy-start
  35.1 0.0 copy-start.1
  35.1 0.1 fusion.26
  35.2 1.3 %collective-permute-start.2 = (f32[9,1,10,1]{3,2,0,1:T(8,128)S(1)}, f32[9,1,10,1]{3,2,0,1:T(8,128)S(1)}, u32[]{:S(2)}, u32[]{:S(2)}) collective-permute-start(f32[9,1,10,1]{3,2,0,1:T(8,128)S(1)} %get-tuple-element.16), channel_id=1, source_target_pairs={{0,1},{2,3},{4,5},{6,7},{8,9},{10,11},{12,13},{14,15},{16,17},{18,... | collective-permute-start | bytes 1088 | tf_op jit(solution)/shard_map/ppermute | solution.py:17
  36.5 4.5 %collective-permute-start.3 = (f32[9,1,10,1]{3,2,0,1:T(8,128)S(1)}, f32[9,1,10,1]{3,2,0,1:T(8,128)S(1)}, u32[]{:S(2)}, u32[]{:S(2)}) collective-permute-start(f32[9,1,10,1]{3,2,0,1:T(8,128)S(1)} %get-tuple-element.17), channel_id=1, source_target_pairs={{1,0},{3,2},{5,4},{7,6},{9,8},{11,10},{13,12},{15,14},{17,16},{19,... | collective-permute-start | bytes 1088 | tf_op jit(solution)/shard_map/ppermute | solution.py:19
  41.0 0.0 copy-done
  41.0 0.0 copy-done.1
  41.1 0.3 convolution_bitcast_fusion.1
  41.3 0.1 copy.13
  41.4 0.0 collective-permute-done.2
  41.4 1.6 %collective-permute-done.3 = f32[9,1,10,1]{3,2,0,1:T(8,128)S(1)} collective-permute-done((f32[9,1,10,1]{3,2,0,1:T(8,128)S(1)}, f32[9,1,10,1]{3,2,0,1:T(8,128)S(1)}, u32[]{:S(2)}, u32[]{:S(2)}) %collective-permute-start.3) | collective-permute-done | bytes 392 | tf_op jit(solution)/shard_map/ppermute | solution.py:19
  43.0 0.2 pad_maximum_fusion
  43.2 0.1 fusion.12
  43.4 0.3 convolution_bitcast_fusion
  43.7 0.1 pad_maximum_fusion.5
  43.8 0.3 convolution_bitcast_fusion.4
  44.0 0.3 convolution_bitcast_fusion.3
  44.4 0.1 or_bitcast_fusion
  44.4 43.8 %all-reduce.1 = (f32[5]{0:T(128)S(1)}, f32[5,5]{1,0:T(8,128)S(1)}, f32[5]{0:T(128)S(1)}, f32[5,5]{0,1:T(8,128)S(1)}) all-reduce(f32[5]{0:T(128)S(1)} %convolution_bitcast_fusion.4, f32[5,5]{1,0:T(8,128)S(1)} %convolution_bitcast_fusion.1, ...), channel_id=1, replica_groups=mesh['shot'=4,'gx'=4,'gy'=2] {'shot','gx','gy'}, use_global_device_ids=true, to_apply=%region_3.0 | all-reduce | flops 60 | bytes 480 | tf_op jit(solution)/shard_map/psum | solution.py:115
  88.3 0.7 fusion.28
  89.0 0.7 fusion.30
  99.2 0.6 gather_fusion
  103.1 0.1 stack.48
  103.2 0.1 fusion
  103.3 0.7 fusion.29
  116.9 0.1 stack.54
  116.9 0.2 fusion.1
  117.2 0.2 fusion.21
  117.4 0.6 negate_bitcast_fusion
  (8 shorter events, 0.2 us)
Async XLA Ops:
  6.5 20.8 %reduce-scatter.4.cloned.1.call-start = ((), (), s32[]{:S(2)}) async-start(), calls=%async_computation.1 | async-start | bytes 184320
  28.2 5.6 %collective-permute-start = (f32[9,1,1,128]{3,2,0,1:T(1,128)S(1)}, f32[9,1,1,128]{3,2,0,1:T(1,128)S(1)}, u32[]{:S(2)}, u32[]{:S(2)}) collective-permute-start(f32[9,1,1,128]{3,2,0,1:T(1,128)S(1)} %get-tuple-element.25), channel_id=1, source_target_pairs={{0,2},{2,4},{4,6},{1,3},{3,5},{5,7},{8,10},{10,12},{12,14},{9,11},... | collective-permute-start | bytes 13832 | tf_op jit(solution)/shard_map/ppermute | solution.py:17
  30.1 5.0 %collective-permute-start.1 = (f32[9,1,1,128]{3,2,0,1:T(1,128)S(1)}, f32[9,1,1,128]{3,2,0,1:T(1,128)S(1)}, u32[]{:S(2)}, u32[]{:S(2)}) collective-permute-start(f32[9,1,1,128]{3,2,0,1:T(1,128)S(1)} %get-tuple-element.26), channel_id=1, source_target_pairs={{2,0},{4,2},{6,4},{3,1},{5,3},{7,5},{10,8},{12,10},{14,12},{11,9},... | collective-permute-start | bytes 13832 | tf_op jit(solution)/shard_map/ppermute | solution.py:19
  35.1 6.0 %copy-start = (f32[5,3,1,8,128]{4,3,2,1,0:T(8,128)S(1)}, f32[5,3,1,8,128]{4,3,2,1,0:T(8,128)}, u32[]{:S(2)}) copy-start(f32[5,3,1,8,128]{4,3,2,1,0:T(8,128)} %param.5) | copy-start | bytes 184324
  35.1 6.0 %copy-start.1 = (f32[5,3,1,8,128]{4,3,2,1,0:T(8,128)S(1)}, f32[5,3,1,8,128]{4,3,2,1,0:T(8,128)}, u32[]{:S(2)}) copy-start(f32[5,3,1,8,128]{4,3,2,1,0:T(8,128)} %param.4) | copy-start | bytes 184324
  35.2 6.2 %collective-permute-start.2 = (f32[9,1,10,1]{3,2,0,1:T(8,128)S(1)}, f32[9,1,10,1]{3,2,0,1:T(8,128)S(1)}, u32[]{:S(2)}, u32[]{:S(2)}) collective-permute-start(f32[9,1,10,1]{3,2,0,1:T(8,128)S(1)} %get-tuple-element.16), channel_id=1, source_target_pairs={{0,1},{2,3},{4,5},{6,7},{8,9},{10,11},{12,13},{14,15},{16,17},{18,... | collective-permute-start | bytes 1088 | tf_op jit(solution)/shard_map/ppermute | solution.py:17
  36.5 6.5 %collective-permute-start.3 = (f32[9,1,10,1]{3,2,0,1:T(8,128)S(1)}, f32[9,1,10,1]{3,2,0,1:T(8,128)S(1)}, u32[]{:S(2)}, u32[]{:S(2)}) collective-permute-start(f32[9,1,10,1]{3,2,0,1:T(8,128)S(1)} %get-tuple-element.17), channel_id=1, source_target_pairs={{1,0},{3,2},{5,4},{7,6},{9,8},{11,10},{13,12},{15,14},{17,16},{19,... | collective-permute-start | bytes 1088 | tf_op jit(solution)/shard_map/ppermute | solution.py:19
Sparse Core Ops, SparseCore 0:
  9.6 17.7 reduce-scatter.3
where the time goes:
time: 126 us; the launch traced here: 125 us
  blocking collectives  43.8 us (35%)
  between operations  39.2 us (31%)
  waiting for transfers between devices  22.1 us (18%)
  starting transfers between devices  11.4 us (9%)
  local copies, waits for them, and re-layouts  4.65 us (4%)
  other arithmetic  1.9 us (2%)
  matrix products  1.73 us (1%)
    psum x1, blocking collectives, per_device(): lax.psum((pair_dots(s_flat, y_flat), curv_part, hist_part, pre_part), ('s...  43.8 us
    unnamed x2, waiting for transfers between devices  19.3 us
    ppermute x2, starting transfers between devices, extended_2(): lax.ppermute(head, axis, [((i + 1) % count, i) for i in range(ends)])  8.19 us
    ppermute x2, starting transfers between devices, extended_2(): lax.ppermute(tail, axis, [(i, (i + 1) % count) for i in range(ends)])  3.21 us
    ppermute x2, waiting for transfers between devices, extended_2(): lax.ppermute(head, axis, [((i + 1) % count, i) for i in range(ends)])  2.87 us
  transfers between devices with their start and end apart: 5, of which 3 were waited for; matrix products, arithmetic and copies ran while one was open for 0% of the time, Pallas kernels for 0%

commit v1 on v0

--- a/solution.py
+++ b/solution.py
@@ -1,9 +1,351 @@
+import functools
+
 import jax
 import jax.numpy as jnp
 from jax import lax
+from jax.experimental import pallas as pl
+from jax.experimental.pallas import tpu as pltpu
 from jax.sharding import PartitionSpec as P
 
 PAIRS = 5
+FIELDS = 9
+AXES = ("shot", "gx", "gy")
+TRI = [(i, j) for i in range(PAIRS) for j in range(i, PAIRS)]
+N_TRI = len(TRI)
+FIRST = -(-N_TRI // 8)
+LATER = -(-(N_TRI + 2 * PAIRS) // 8)
+GROUPS = FIRST + LATER
+BESIDE = FIELDS
+HISTORY = 2 * FIELDS
+HALF = 64
+LIMIT = 4 << 20
+SORDER = (2, 3, 1)
+STAGES = [[{'gx': 1}], [{'gx': 3}], [{'shot': 3, 'gx': 1}, {'shot': 2, 'gx': 1}, {'shot': 1, 'gx': 1}]]
+
+
+VMEM = pl.BlockSpec(memory_space=pltpu.VMEM)
+
+
+def call(kernel, out_shapes, args, scratch=()):
+    out = [jax.ShapeDtypeStruct(shape, jnp.float32) for shape in out_shapes]
+    return pl.pallas_call(
+        kernel,
+        out_shape=out,
+        in_specs=[VMEM] * len(args),
+        out_specs=[VMEM] * len(out),
+        scratch_shapes=[pltpu.VMEM(shape, jnp.float32) for shape in scratch],
+        compiler_params=pltpu.CompilerParams(vmem_limit_bytes=LIMIT),
+    )(*args)
+
+
+def iota(shape, dim):
+    return lax.broadcasted_iota(jnp.int32, shape, dim)
+
+
+def edge_lane(width):
+    first = lax.axis_index("gy") == 0
+    return jnp.where(first, width - 1, 0), jnp.where(first, -1, 1)
+
+
+def dot(a, b):
+    return a[0] * b[0] + a[1] * b[1] + a[2] * b[2]
+
+
+def inverse(hessian):
+    diag_p, diag_s, diag_r, cross_ps, cross_pr, cross_sr = hessian
+    cof_pp = diag_s * diag_r - cross_sr * cross_sr
+    cof_ps = cross_pr * cross_sr - cross_ps * diag_r
+    cof_pr = cross_ps * cross_sr - diag_s * cross_pr
+    cof_ss = diag_p * diag_r - cross_pr * cross_pr
+    cof_sr = cross_ps * cross_pr - diag_p * cross_sr
+    cof_rr = diag_p * diag_s - cross_ps * cross_ps
+    determinant = diag_p * cof_pp + cross_ps * cof_ps + cross_pr * cof_pr
+    inverse_det = 1.0 / determinant
+    return [c * inverse_det for c in (cof_pp, cof_ps, cof_pr, cof_ss, cof_sr, cof_rr)]
+
+
+def applied(inv, vec):
+    one, two, three = vec
+    return [
+        inv[0] * one + inv[1] * two + inv[2] * three,
+        inv[1] * one + inv[3] * two + inv[4] * three,
+        inv[2] * one + inv[4] * two + inv[5] * three,
+    ]
+
+
+def later_sums(smooth, s, y):
+    grad = smooth[0:3]
+    inv = inverse(smooth[3:9])
+    newton = applied(inv, grad)
+    terms = [None] * (N_TRI + 2 * PAIRS)
+    for j in range(PAIRS):
+        z = applied(inv, y[j])
+        for i in range(j + 1):
+            terms[TRI.index((i, j))] = dot(y[i], z)
+        terms[N_TRI + j] = dot(s[j], grad)
+        terms[N_TRI + PAIRS + j] = dot(y[j], newton)
+    return terms
+
+
+def added(sums, terms):
+    return terms if sums is None else [a + b for a, b in zip(sums, terms)]
+
+
+def packed_sums(sums, slots, group):
+    rows, width = sums[0].shape
+    groups = -(-len(sums) // 8)
+    for k in range(8 * groups):
+        slots[k * rows : (k + 1) * rows] = sums[k] if k < len(sums) else jnp.zeros((rows, width))
+    lane = iota((8, width), 1)
+    packed = jnp.zeros((8, width), jnp.float32)
+    for g in range(groups):
+        total = slots[pl.ds(g * 8 * rows, 8, stride=rows)]
+        for r in range(1, rows):
+            total = total + slots[pl.ds(g * 8 * rows + r, 8, stride=rows)]
+        packed = jnp.where(lane == group + g, jnp.sum(total, axis=1, keepdims=True), packed)
+    return packed
+
+
+def history_kernel(s_ref, y_ref, column_ref, part_ref, slots):
+    levels, rows, width = s_ref.shape[2:]
+    edge, _ = edge_lane(width)
+    lane = iota((rows, width), 1)
+    sums = None
+    for level in range(levels):
+        s = [[s_ref[i, p, level] for p in range(3)] for i in range(PAIRS)]
+        y = [[y_ref[i, p, level] for p in range(3)] for i in range(PAIRS)]
+        column = jnp.zeros((rows, width), jnp.float32)
+        for k, value in enumerate(sum(s, []) + sum(y, [])):
+            at = HISTORY + k
+            column = jnp.where(lane == at, pltpu.roll(value, (at + width - edge) % width, 1), column)
+        column_ref[level] = column
+        sums = added(sums, [dot(s[i], y[j]) for i, j in TRI])
+    part_ref[...] = packed_sums(sums, slots, 0)
+
+
+def sum_kernel(scale, count, *refs):
+    blocks, (fields_ref, first_ref, last_ref) = refs[:count], refs[count:]
+    levels, rows = fields_ref.shape[1:3]
+    for level in range(levels):
+        for f in range(FIELDS):
+            total = blocks[0][f, level]
+            for block in blocks[1:]:
+                total = total + block[f, level]
+            total = total * scale
+            fields_ref[f, level] = total
+            first_ref[level, f : f + 1] = total[0:1]
+            last_ref[level, f : f + 1] = total[rows - 1 : rows]
+
+
+def along_y(own, halo=None):
+    width = own.shape[-1]
+    lane = iota(own.shape, 1)
+    left = jnp.where(lane == 0, 0.0, pltpu.roll(own, 1, 1))
+    right = jnp.where(lane == width - 1, 0.0, pltpu.roll(own, width - 1, 1))
+    if halo is not None:
+        left = left + halo
+    return 0.25 * (left + 2.0 * own + right)
+
+
+def main_kernel(
+    fields_ref, above_ref, below_ref, s_ref, y_ref, column_ref, cross_ref, along_ref, send_ref, slots
+):
+    levels, rows, width = fields_ref.shape[1:]
+    edge, step = edge_lane(width)
+    sub = iota((rows, width), 0)
+    lane = iota((rows, width), 1)
+    at = lax.axis_index("gx")
+    has_above = at > 0
+    has_below = at < lax.axis_size("gx") - 1
+    sums = None
+    for level in range(levels):
+        column = column_ref[level]
+        smooth = []
+        for f in range(FIELDS):
+            own = fields_ref[f, level]
+            above = jnp.where(has_above, above_ref[level, f : f + 1], 0.0)
+            below = jnp.where(has_below, below_ref[level, f : f + 1], 0.0)
+            up = jnp.where(sub == 0, jnp.broadcast_to(above, own.shape), pltpu.roll(own, 1, 0))
+            down = jnp.where(
+                sub == rows - 1, jnp.broadcast_to(below, own.shape), pltpu.roll(own, rows - 1, 0)
+            )
+            value = 0.25 * (up + 2.0 * own + down)
+            along_ref[f, level] = value
+            moved = pltpu.roll(value, (f + width - edge) % width, 1)
+            column = jnp.where(lane == f, moved, column)
+            moved = pltpu.roll(value, (BESIDE + f + width - edge - step) % width, 1)
+            column = jnp.where(lane == BESIDE + f, moved, column)
+            smooth.append(along_y(value))
+        send_ref[level] = column
+        s = [[s_ref[i, p, level] for p in range(3)] for i in range(PAIRS)]
+        y = [[y_ref[i, p, level] for p in range(3)] for i in range(PAIRS)]
+        sums = added(sums, later_sums(smooth, s, y))
+    inside = lane != edge
+    sums = [jnp.where(inside, total, 0.0) for total in sums]
+    send_ref[levels] = cross_ref[...] + packed_sums(sums, slots, FIRST)
+
+
+def edge_kernel(own_ref, other_ref, part_ref, slots):
+    levels, rows, width = own_ref.shape
+    levels -= 1
+    lane = iota((rows, width), 1)
+    sums = None
+    for level in range(levels):
+        own, other = own_ref[level], other_ref[level]
+        own_edge = 0.25 * (pltpu.roll(own, width - BESIDE, 1) + 2.0 * own + other)
+        other_edge = 0.25 * (pltpu.roll(other, width - BESIDE, 1) + 2.0 * other + own)
+        fields = jnp.where(lane < HALF, own_edge, pltpu.roll(other_edge, HALF, 1))
+        history = jnp.where(lane < HALF, own, pltpu.roll(other, HALF, 1))
+
+        def entry(array, k):
+            return array if k == 0 else pltpu.roll(array, width - k, 1)
+
+        smooth = [entry(fields, f) for f in range(FIELDS)]
+        vectors = [entry(history, HISTORY + k) for k in range(6 * PAIRS)]
+        vectors = [vectors[k : k + 3] for k in range(0, 6 * PAIRS, 3)]
+        sums = added(sums, later_sums(smooth, vectors[:PAIRS], vectors[PAIRS:]))
+    cells = jnp.logical_or(lane == 0, lane == HALF)
+    sums = [jnp.where(cells, total, 0.0) for total in sums]
+    part_ref[...] = own_ref[levels] + other_ref[levels] + packed_sums(sums, slots, FIRST)
+
+
+def cells_kernel(along_ref, other_ref, cells_ref):
+    levels, rows, width = along_ref.shape[1:]
+    edge, _ = edge_lane(width)
+    lane = iota((rows, width), 1)
+    for level in range(levels):
+        smooth = []
+        for f in range(FIELDS):
+            moved = pltpu.roll(other_ref[level], (edge + width - f) % width, 1)
+            smooth.append(along_y(along_ref[f, level], jnp.where(lane == edge, moved, 0.0)))
+        for k, value in enumerate(smooth[0:3] + inverse(smooth[3:9])):
+            cells_ref[k, level] = value
+
+
+def combine_kernel(count, *refs):
+    parts, (cells_ref, s_ref, y_ref, out_ref, spread_ref) = refs[:count], refs[count:]
+    levels, rows, width = s_ref.shape[2:]
+    packed = parts[0][...]
+    for part in parts[1:]:
+        packed = packed + part[...]
+    for g in range(GROUPS):
+        spread_ref[g * 8 : (g + 1) * 8] = jnp.broadcast_to(packed[:, g : g + 1], (8, width))
+
+    def entry(k, group=0):
+        return spread_ref[8 * group + k : 8 * group + k + 1]
+
+    cross = {pair: entry(k) for k, pair in enumerate(TRI)}
+    curv = {pair: entry(k, FIRST) for k, pair in enumerate(TRI)}
+    hist_dot = [entry(N_TRI + i, FIRST) for i in range(PAIRS)]
+    pre_dot = [entry(N_TRI + PAIRS + i, FIRST) for i in range(PAIRS)]
+    scale = [1.0 / cross[i, i] for i in range(PAIRS)]
+    coef_p = [None] * PAIRS
+    for row in range(PAIRS - 1, -1, -1):
+        total = hist_dot[row]
+        for col in range(PAIRS - 1, row, -1):
+            total = total - cross[row, col] * coef_p[col]
+        coef_p[row] = total * scale[row]
+    coef_q = [None] * PAIRS
+    for row in range(PAIRS):
+        total = cross[row, row] * coef_p[row] - pre_dot[row]
+        for col in range(PAIRS):
+            total = total + curv[min(row, col), max(row, col)] * coef_p[col]
+        for col in range(row):
+            total = total - cross[col, row] * coef_q[col]
+        coef_q[row] = total * scale[row]
+    coef_p = [jnp.broadcast_to(c, (rows, width)) for c in coef_p]
+    coef_q = [jnp.broadcast_to(c, (rows, width)) for c in coef_q]
+    for level in range(levels):
+        rest = []
+        for p in range(3):
+            total = cells_ref[p, level]
+            for i in range(PAIRS):
+                total = total - coef_p[i] * y_ref[i, p, level]
+            rest.append(total)
+        solved = applied([cells_ref[3 + k, level] for k in range(6)], rest)
+        for p in range(3):
+            total = solved[p]
+            for i in range(PAIRS):
+                total = total + coef_q[i] * s_ref[i, p, level]
+            out_ref[p, level] = -total
+
+
+def flipped(x, flips):
+    sizes = [lax.axis_size(a) for a in AXES]
+    pairs = []
+    for i in range(sizes[0]):
+        for j in range(sizes[1]):
+            for k in range(sizes[2]):
+                to = [a ^ flips.get(n, 0) for n, a in zip(AXES, (i, j, k))]
+                pairs.append(
+                    (
+                        (i * sizes[1] + j) * sizes[2] + k,
+                        (to[0] * sizes[1] + to[1]) * sizes[2] + to[2],
+                    )
+                )
+    return lax.ppermute(x, AXES, pairs)
+
+
+def shot_blocks(partials):
+    n = lax.axis_size("shot")
+    levels = partials.shape[1] // n
+    me = lax.axis_index("shot")
+
+    def block(k):
+        return lax.dynamic_slice_in_dim(partials, (me ^ k) * levels, levels, axis=1)
+
+    mine = [block(k) for k in range(n)]
+    blocks = [mine[0]]
+    for k in SORDER:
+        blocks.append(flipped(mine[k], {"shot": k}))
+    return blocks
+
+
+def all_sums(part):
+    pieces = [part]
+    for stage in STAGES:
+        part = functools.reduce(jnp.add, pieces)
+        pieces = [part]
+        for flip in stage:
+            pieces.append(flipped(part, flip))
+    return pieces
+
+
+def exchanged(partials, hist_s, hist_y):
+    levels, rows, width = hist_s.shape[2:]
+    scale = 1.0 / lax.axis_size("shot")
+    n_x = lax.axis_size("gx")
+    tile = (FIELDS, levels, rows, width)
+    edge = (levels, FIELDS, width)
+    blocks = shot_blocks(partials[0])
+    column, cross = call(
+        history_kernel,
+        [(levels, rows, width), (8, width)],
+        [hist_s, hist_y],
+        [(8 * FIRST * rows, width)],
+    )
+    fields, first, last = call(
+        functools.partial(sum_kernel, scale, len(blocks)), [tile, edge, edge], blocks
+    )
+    above = lax.ppermute(last, "gx", [(i, (i + 1) % n_x) for i in range(n_x)])
+    below = lax.ppermute(first, "gx", [((i + 1) % n_x, i) for i in range(n_x)])
+    along, send = call(
+        main_kernel,
+        [tile, (levels + 1, rows, width)],
+        [fields, above, below, hist_s, hist_y, column, cross],
+        [(8 * LATER * rows, width)],
+    )
+    other = flipped(send, {"gy": 1})
+    (part,) = call(edge_kernel, [(rows, width)], [send, other], [(8 * LATER * rows, width)])
+    (cells,) = call(cells_kernel, [tile], [along, other])
+    pieces = all_sums(part)
+    (direction,) = call(
+        functools.partial(combine_kernel, len(pieces)),
+        [(3, levels, rows, width)],
+        pieces + [cells, hist_s, hist_y],
+        [(8 * GROUPS, width)],
+    )
+    return direction
 
 
 def extended_2(cells, sides, width):
@@ -98,7 +440,7 @@
     return -(solved[0] + update_s - update_z)
 
 
-def per_device(partials, hist_s, hist_y):
+def plain_device(partials, hist_s, hist_y):
     s_flat = hist_s.reshape(PAIRS, -1)
     y_flat = hist_y.reshape(PAIRS, -1)
     inverse_count = 1.0 / lax.axis_size("shot")
@@ -118,9 +460,15 @@
     return combine_terms(cross_gram, curv_gram, hist_dot, pre_dot, solved, hist_s)
 
 
+def per_device(*args):
+    return exchanged(*args)
+
+
 def solution(mesh):
+    sizes = [mesh.shape[a] for a in AXES]
+    fits = sizes[0] == 4 and sizes[1] == 4 and sizes[2] == 2
     return jax.shard_map(
-        per_device,
+        per_device if fits else plain_device,
         mesh=mesh,
         in_specs=(
             P("shot", None, None, "gx", "gy"),

time: 126 us -> 29.7 us (0.24)
  the two profiles are of different devices: /device:TPU:14 before, /device:TPU:0 now
where the time goes in v1:
time: 29.7 us; the launch traced here: 29.6 us
  starting transfers between devices  13.8 us (46%)
  waiting for transfers between devices  13.3 us (45%)
  Pallas kernels  1.6 us (5%)
  local copies, waits for them, and re-layouts  0.84 us (3%)
    ppermute x9, waiting for transfers between devices, flipped(): return lax.ppermute(x, AXES, pairs)  12.1 us
    ppermute x9, starting transfers between devices, flipped(): return lax.ppermute(x, AXES, pairs)  12 us
    ppermute x1, starting transfers between devices, exchanged(): below = lax.ppermute(first, 'gx', [((i + 1) % n_x, i) for i in range(n_x)])  1.73 us
    pallas_call x6, Pallas kernels, call(): pl.pallas_call(kernel, out_shape=out, in_specs=[VMEM] * len(args), out_sp...  1.6 us
    ppermute x1, waiting for transfers between devices, exchanged(): above = lax.ppermute(last, 'gx', [(i, (i + 1) % n_x) for i in range(n_x)])  1.17 us
    dynamic_slice x1, local copies, waits for them, and re-layouts, block(): return lax.dynamic_slice_in_dim(partials, (me ^ k) * levels, levels, axis=1)  0.83 us
  transfers between devices with their start and end apart: 11, of which 8 were waited for; matrix products, arithmetic and copies ran while one was open for 0% of the time, Pallas kernels for 1%

profile of v1, /device:TPU:0, one launch (start us, length us, event | category | flops | bytes accessed | tf_op | source)
XLA Modules:
  0.0 29.6 jit_solution(16084009463251394938)
XLA Ops:
  0.0 0.8 %dynamic-slice_bitcast_fusion = (f32[9,1,8,128]{3,2,1,0:T(8,128)S(1)}, f32[9,1,8,128]{3,2,1,0:T(8,128)S(1)}, f32[9,1,8,128]{3,2,1,0:T(8,128)S(1)}, f32[9,1,8,128]{3,2,1,0:T(8,128)S(1)}) fusion(f32[1,9,4,8,128]{4,3,2,1,0:T(8,128)} %param.3, s32[]{:T(128)S(6)} %select_n.15, s32[]{:T(128)S(6)} %select_n.13, s32[]{:T(128)S(6)} %select_n.12, s32[]{:T(128)S(6)} %select_n.14), kind=kLoop, calls=%fused_computation | loop fusion | bytes 294928 | tf_op jit(solution)/shard_map/dynamic_slice | solution.py:295
  0.8 4.1 %collective-permute-start = (f32[9,1,8,128]{3,2,1,0:T(8,128)S(1)}, f32[9,1,8,128]{3,2,1,0:T(8,128)S(1)}, u32[]{:S(2)}, u32[]{:S(2)}) collective-permute-start(f32[9,1,8,128]{3,2,1,0:T(8,128)S(1)} %get-tuple-element.20), channel_id=1, source_target_pairs={{0,16},{1,17},{2,18},{3,19},{4,20},{5,21},{6,22},{7,23},{8,24},{9,... | collective-permute-start | bytes 110600 | tf_op jit(solution)/shard_map/ppermute | solution.py:286
  5.0 1.3 %collective-permute-start.1 = (f32[9,1,8,128]{3,2,1,0:T(8,128)S(1)}, f32[9,1,8,128]{3,2,1,0:T(8,128)S(1)}, u32[]{:S(2)}, u32[]{:S(2)}) collective-permute-start(f32[9,1,8,128]{3,2,1,0:T(8,128)S(1)} %get-tuple-element.22), channel_id=1, source_target_pairs={{0,24},{1,25},{2,26},{3,27},{4,28},{5,29},{6,30},{7,31},{8,16},{9,... | collective-permute-start | bytes 110600 | tf_op jit(solution)/shard_map/ppermute | solution.py:286
  6.3 0.2 collective-permute-start.2
  6.5 0.8 %collective-permute-done.refs_1_ = f32[9,1,8,128]{3,2,1,0:T(8,128)S(1)} collective-permute-done((f32[9,1,8,128]{3,2,1,0:T(8,128)S(1)}, f32[9,1,8,128]{3,2,1,0:T(8,128)S(1)}, u32[]{:S(2)}, u32[]{:S(2)}) %collective-permute-start) | collective-permute-done | bytes 36896 | tf_op jit(solution)/shard_map/ppermute | solution.py:286
  7.3 3.4 %collective-permute-done.1.refs_2_ = f32[9,1,8,128]{3,2,1,0:T(8,128)S(1)} collective-permute-done((f32[9,1,8,128]{3,2,1,0:T(8,128)S(1)}, f32[9,1,8,128]{3,2,1,0:T(8,128)S(1)}, u32[]{:S(2)}, u32[]{:S(2)}) %collective-permute-start.1) | collective-permute-done | bytes 36896 | tf_op jit(solution)/shard_map/ppermute | solution.py:286
  10.7 0.0 collective-permute-done.2.refs_3_
  10.7 0.0 copy-start
  10.7 0.0 copy-start.1
  10.8 0.1 collective-permute-start.3
  10.8 1.7 %collective-permute-start.4 = (f32[1,9,128]{2,1,0:T(8,128)S(1)}, f32[1,9,128]{2,1,0:T(8,128)S(1)}, u32[]{:S(2)}, u32[]{:S(2)}) collective-permute-start(f32[1,9,128]{2,1,0:T(8,128)S(1)} %get-tuple-element.14), channel_id=1, source_target_pairs={{2,0},{4,2},{6,4},{0,6},{3,1},{5,3},{7,5},{1,7},{10,8},{12,10},{14... | collective-permute-start | bytes 13832 | tf_op jit(solution)/shard_map/ppermute | solution.py:331
  12.5 0.0 copy-done
  12.6 0.0 copy-done.1
  12.6 0.2 shard_map.38
  12.7 1.2 %collective-permute-done.3.above_ref = f32[1,9,128]{2,1,0:T(8,128)S(1)} collective-permute-done((f32[1,9,128]{2,1,0:T(8,128)S(1)}, f32[1,9,128]{2,1,0:T(8,128)S(1)}, u32[]{:S(2)}, u32[]{:S(2)}) %collective-permute-start.3) | collective-permute-done | bytes 4640 | tf_op jit(solution)/shard_map/ppermute | solution.py:330
  13.9 0.0 collective-permute-done.4.below_ref
  13.9 0.2 shard_map.39
  14.1 1.6 %collective-permute-start.5 = (f32[2,8,128]{2,1,0:T(8,128)S(1)}, f32[2,8,128]{2,1,0:T(8,128)S(1)}, u32[]{:S(2)}, u32[]{:S(2)}) collective-permute-start(f32[2,8,128]{2,1,0:T(8,128)S(1)} %get-tuple-element.17.own_ref), channel_id=1, source_target_pairs={{0,1},{1,0},{2,3},{3,2},{4,5},{5,4},{6,7},{7,6},{8,9},{9,8},{10,11... | collective-permute-start | bytes 24584 | tf_op jit(solution)/shard_map/ppermute | solution.py:286
  15.7 2.1 %collective-permute-done.5.other_ref = f32[2,8,128]{2,1,0:T(8,128)S(1)} collective-permute-done((f32[2,8,128]{2,1,0:T(8,128)S(1)}, f32[2,8,128]{2,1,0:T(8,128)S(1)}, u32[]{:S(2)}, u32[]{:S(2)}) %collective-permute-start.5) | collective-permute-done | bytes 8224 | tf_op jit(solution)/shard_map/ppermute | solution.py:286
  17.8 0.4 %shard_map.40 = f32[8,128]{1,0:T(8,128)S(1)} custom-call(f32[2,8,128]{2,1,0:T(8,128)S(1)} %get-tuple-element.17.own_ref, f32[2,8,128]{2,1,0:T(8,128)S(1)} %collective-permute-done.5.other_ref), custom_call_target="tpu_custom_call" | custom-call | tf_op jit(solution)/shard_map/pallas_call | solution.py:31
  18.2 0.4 %collective-permute-start.6 = (f32[8,128]{1,0:T(8,128)S(1)}, f32[8,128]{1,0:T(8,128)S(1)}, u32[]{:S(2)}, u32[]{:S(2)}) collective-permute-start(f32[8,128]{1,0:T(8,128)S(1)} %shard_map.40), channel_id=1, source_target_pairs={{0,2},{1,3},{2,0},{3,1},{4,6},{5,7},{6,4},{7,5},{8,10},{9,11},{10,... | collective-permute-start | bytes 12296 | tf_op jit(solution)/shard_map/ppermute | solution.py:286
  18.6 0.8 %collective-permute-done.6 = f32[8,128]{1,0:T(8,128)S(1)} collective-permute-done((f32[8,128]{1,0:T(8,128)S(1)}, f32[8,128]{1,0:T(8,128)S(1)}, u32[]{:S(2)}, u32[]{:S(2)}) %collective-permute-start.6) | collective-permute-done | bytes 4128 | tf_op jit(solution)/shard_map/ppermute | solution.py:286
  19.5 1.2 %collective-permute-start.7 = (f32[8,128]{1,0:T(8,128)S(1)}, f32[8,128]{1,0:T(8,128)S(1)}, u32[]{:S(2)}, u32[]{:S(2)}) collective-permute-start(f32[8,128]{1,0:T(8,128)S(1)} %add.22), channel_id=1, source_target_pairs={{0,6},{1,7},{2,4},{3,5},{4,2},{5,3},{6,0},{7,1},{8,14},{9,15},{10,... | collective-permute-start | bytes 12296 | tf_op jit(solution)/shard_map/ppermute | solution.py:286
  20.6 1.8 %collective-permute-done.7 = f32[8,128]{1,0:T(8,128)S(1)} collective-permute-done((f32[8,128]{1,0:T(8,128)S(1)}, f32[8,128]{1,0:T(8,128)S(1)}, u32[]{:S(2)}, u32[]{:S(2)}) %collective-permute-start.7) | collective-permute-done | bytes 4128 | tf_op jit(solution)/shard_map/ppermute | solution.py:286
  22.5 0.0 collective-permute-start.10
  22.5 2.4 %collective-permute-start.8 = (f32[8,128]{1,0:T(8,128)S(1)}, f32[8,128]{1,0:T(8,128)S(1)}, u32[]{:S(2)}, u32[]{:S(2)}) collective-permute-start(f32[8,128]{1,0:T(8,128)S(1)} %add.23.refs_0_), channel_id=1, source_target_pairs={{0,26},{1,27},{2,24},{3,25},{4,30},{5,31},{6,28},{7,29},{8,18},{9,... | collective-permute-start | bytes 12296 | tf_op jit(solution)/shard_map/ppermute | solution.py:286
  24.9 0.7 %collective-permute-start.9 = (f32[8,128]{1,0:T(8,128)S(1)}, f32[8,128]{1,0:T(8,128)S(1)}, u32[]{:S(2)}, u32[]{:S(2)}) collective-permute-start(f32[8,128]{1,0:T(8,128)S(1)} %add.23.refs_0_), channel_id=1, source_target_pairs={{0,18},{1,19},{2,16},{3,17},{4,22},{5,23},{6,20},{7,21},{8,26},{9,... | collective-permute-start | bytes 12296 | tf_op jit(solution)/shard_map/ppermute | solution.py:286
  25.6 0.1 shard_map.41.refs_4_
  25.8 0.0 collective-permute-done.10.refs_3_
  25.8 1.6 %collective-permute-done.8.refs_1_ = f32[8,128]{1,0:T(8,128)S(1)} collective-permute-done((f32[8,128]{1,0:T(8,128)S(1)}, f32[8,128]{1,0:T(8,128)S(1)}, u32[]{:S(2)}, u32[]{:S(2)}) %collective-permute-start.8) | collective-permute-done | bytes 4128 | tf_op jit(solution)/shard_map/ppermute | solution.py:286
  27.3 1.5 %collective-permute-done.9.refs_2_ = f32[8,128]{1,0:T(8,128)S(1)} collective-permute-done((f32[8,128]{1,0:T(8,128)S(1)}, f32[8,128]{1,0:T(8,128)S(1)}, u32[]{:S(2)}, u32[]{:S(2)}) %collective-permute-start.9) | collective-permute-done | bytes 4128 | tf_op jit(solution)/shard_map/ppermute | solution.py:286
  28.8 0.7 %shard_map.42 = f32[3,1,8,128]{3,2,1,0:T(8,128)} custom-call(f32[8,128]{1,0:T(8,128)S(1)} %add.23.refs_0_, f32[8,128]{1,0:T(8,128)S(1)} %collective-permute-done.8.refs_1_, f32[8,128]{1,0:T(8,128)S(1)} %collective-permute-done.9.refs_2_, f32[8,128]{1,0:T(8,128)S(1)} %collective-permute-done.10.refs_3_, f32[9,1,8,128]{3,2,1,0:T(8,128)S(1)} %shard_map.41.refs_4_, ...), custom_call_target="tpu_custom_call" | custom-call | tf_op jit(solution)/shard_map/pallas_call | solution.py:31
  (3 shorter events, 0.0 us)
Async XLA Ops:
  0.8 6.5 %collective-permute-start = (f32[9,1,8,128]{3,2,1,0:T(8,128)S(1)}, f32[9,1,8,128]{3,2,1,0:T(8,128)S(1)}, u32[]{:S(2)}, u32[]{:S(2)}) collective-permute-start(f32[9,1,8,128]{3,2,1,0:T(8,128)S(1)} %get-tuple-element.20), channel_id=1, source_target_pairs={{0,16},{1,17},{2,18},{3,19},{4,20},{5,21},{6,22},{7,23},{8,24},{9,... | collective-permute-start | bytes 110600 | tf_op jit(solution)/shard_map/ppermute | solution.py:286
  5.0 5.8 %collective-permute-start.1 = (f32[9,1,8,128]{3,2,1,0:T(8,128)S(1)}, f32[9,1,8,128]{3,2,1,0:T(8,128)S(1)}, u32[]{:S(2)}, u32[]{:S(2)}) collective-permute-start(f32[9,1,8,128]{3,2,1,0:T(8,128)S(1)} %get-tuple-element.22), channel_id=1, source_target_pairs={{0,24},{1,25},{2,26},{3,27},{4,28},{5,29},{6,30},{7,31},{8,16},{9,... | collective-permute-start | bytes 110600 | tf_op jit(solution)/shard_map/ppermute | solution.py:286
  6.3 4.4 %collective-permute-start.2 = (f32[9,1,8,128]{3,2,1,0:T(8,128)S(1)}, f32[9,1,8,128]{3,2,1,0:T(8,128)S(1)}, u32[]{:S(2)}, u32[]{:S(2)}) collective-permute-start(f32[9,1,8,128]{3,2,1,0:T(8,128)S(1)} %get-tuple-element.19), channel_id=1, source_target_pairs={{0,8},{1,9},{2,10},{3,11},{4,12},{5,13},{6,14},{7,15},{8,0},{9,1},... | collective-permute-start | bytes 110600 | tf_op jit(solution)/shard_map/ppermute | solution.py:286
  10.7 1.8 %copy-start = (f32[5,3,1,8,128]{4,3,2,1,0:T(8,128)S(1)}, f32[5,3,1,8,128]{4,3,2,1,0:T(8,128)}, u32[]{:S(2)}) copy-start(f32[5,3,1,8,128]{4,3,2,1,0:T(8,128)} %refs_5_.1) | copy-start | bytes 184324
  10.7 1.8 %copy-start.1 = (f32[5,3,1,8,128]{4,3,2,1,0:T(8,128)S(1)}, f32[5,3,1,8,128]{4,3,2,1,0:T(8,128)}, u32[]{:S(2)}) copy-start(f32[5,3,1,8,128]{4,3,2,1,0:T(8,128)} %refs_6_.1) | copy-start | bytes 184324
  10.8 3.1 %collective-permute-start.3 = (f32[1,9,128]{2,1,0:T(8,128)S(1)}, f32[1,9,128]{2,1,0:T(8,128)S(1)}, u32[]{:S(2)}, u32[]{:S(2)}) collective-permute-start(f32[1,9,128]{2,1,0:T(8,128)S(1)} %get-tuple-element.13), channel_id=1, source_target_pairs={{0,2},{2,4},{4,6},{6,0},{1,3},{3,5},{5,7},{7,1},{8,10},{10,12},{12... | collective-permute-start | bytes 13832 | tf_op jit(solution)/shard_map/ppermute | solution.py:330
  10.8 3.1 %collective-permute-start.4 = (f32[1,9,128]{2,1,0:T(8,128)S(1)}, f32[1,9,128]{2,1,0:T(8,128)S(1)}, u32[]{:S(2)}, u32[]{:S(2)}) collective-permute-start(f32[1,9,128]{2,1,0:T(8,128)S(1)} %get-tuple-element.14), channel_id=1, source_target_pairs={{2,0},{4,2},{6,4},{0,6},{3,1},{5,3},{7,5},{1,7},{10,8},{12,10},{14... | collective-permute-start | bytes 13832 | tf_op jit(solution)/shard_map/ppermute | solution.py:331
  14.1 3.7 %collective-permute-start.5 = (f32[2,8,128]{2,1,0:T(8,128)S(1)}, f32[2,8,128]{2,1,0:T(8,128)S(1)}, u32[]{:S(2)}, u32[]{:S(2)}) collective-permute-start(f32[2,8,128]{2,1,0:T(8,128)S(1)} %get-tuple-element.17.own_ref), channel_id=1, source_target_pairs={{0,1},{1,0},{2,3},{3,2},{4,5},{5,4},{6,7},{7,6},{8,9},{9,8},{10,11... | collective-permute-start | bytes 24584 | tf_op jit(solution)/shard_map/ppermute | solution.py:286
  18.2 1.2 %collective-permute-start.6 = (f32[8,128]{1,0:T(8,128)S(1)}, f32[8,128]{1,0:T(8,128)S(1)}, u32[]{:S(2)}, u32[]{:S(2)}) collective-permute-start(f32[8,128]{1,0:T(8,128)S(1)} %shard_map.40), channel_id=1, source_target_pairs={{0,2},{1,3},{2,0},{3,1},{4,6},{5,7},{6,4},{7,5},{8,10},{9,11},{10,... | collective-permute-start | bytes 12296 | tf_op jit(solution)/shard_map/ppermute | solution.py:286
  19.5 3.0 %collective-permute-start.7 = (f32[8,128]{1,0:T(8,128)S(1)}, f32[8,128]{1,0:T(8,128)S(1)}, u32[]{:S(2)}, u32[]{:S(2)}) collective-permute-start(f32[8,128]{1,0:T(8,128)S(1)} %add.22), channel_id=1, source_target_pairs={{0,6},{1,7},{2,4},{3,5},{4,2},{5,3},{6,0},{7,1},{8,14},{9,15},{10,... | collective-permute-start | bytes 12296 | tf_op jit(solution)/shard_map/ppermute | solution.py:286
  22.5 3.3 %collective-permute-start.10 = (f32[8,128]{1,0:T(8,128)S(1)}, f32[8,128]{1,0:T(8,128)S(1)}, u32[]{:S(2)}, u32[]{:S(2)}) collective-permute-start(f32[8,128]{1,0:T(8,128)S(1)} %add.23.refs_0_), channel_id=1, source_target_pairs={{0,10},{1,11},{2,8},{3,9},{4,14},{5,15},{6,12},{7,13},{8,2},{9,3},... | collective-permute-start | bytes 12296 | tf_op jit(solution)/shard_map/ppermute | solution.py:286
  22.5 4.8 %collective-permute-start.8 = (f32[8,128]{1,0:T(8,128)S(1)}, f32[8,128]{1,0:T(8,128)S(1)}, u32[]{:S(2)}, u32[]{:S(2)}) collective-permute-start(f32[8,128]{1,0:T(8,128)S(1)} %add.23.refs_0_), channel_id=1, source_target_pairs={{0,26},{1,27},{2,24},{3,25},{4,30},{5,31},{6,28},{7,29},{8,18},{9,... | collective-permute-start | bytes 12296 | tf_op jit(solution)/shard_map/ppermute | solution.py:286
  24.9 3.9 %collective-permute-start.9 = (f32[8,128]{1,0:T(8,128)S(1)}, f32[8,128]{1,0:T(8,128)S(1)}, u32[]{:S(2)}, u32[]{:S(2)}) collective-permute-start(f32[8,128]{1,0:T(8,128)S(1)} %add.23.refs_0_), channel_id=1, source_target_pairs={{0,18},{1,19},{2,16},{3,17},{4,22},{5,23},{6,20},{7,21},{8,26},{9,... | collective-permute-start | bytes 12296 | tf_op jit(solution)/shard_map/ppermute | solution.py:286

commit v2 on v1

--- a/solution.py
+++ b/solution.py
@@ -16,11 +16,9 @@
 LATER = -(-(N_TRI + 2 * PAIRS) // 8)
 GROUPS = FIRST + LATER
 BESIDE = FIELDS
-HISTORY = 2 * FIELDS
-HALF = 64
+SUMS = 2 * FIELDS
+BLOCK = 32
 LIMIT = 4 << 20
-SORDER = (2, 3, 1)
-STAGES = [[{'gx': 1}], [{'gx': 3}], [{'shot': 3, 'gx': 1}, {'shot': 2, 'gx': 1}, {'shot': 1, 'gx': 1}]]
 
 
 VMEM = pl.BlockSpec(memory_space=pltpu.VMEM)
@@ -45,6 +43,10 @@
 def edge_lane(width):
     first = lax.axis_index("gy") == 0
     return jnp.where(first, width - 1, 0), jnp.where(first, -1, 1)
+
+
+def block_lane():
+    return BLOCK * (2 * lax.axis_index("gy") + lax.axis_index("gx") % 2)
 
 
 def dot(a, b):
@@ -98,6 +100,7 @@
         slots[k * rows : (k + 1) * rows] = sums[k] if k < len(sums) else jnp.zeros((rows, width))
     lane = iota((8, width), 1)
     packed = jnp.zeros((8, width), jnp.float32)
+    group = group + SUMS
     for g in range(groups):
         total = slots[pl.ds(g * 8 * rows, 8, stride=rows)]
         for r in range(1, rows):
@@ -109,6 +112,7 @@
 def history_kernel(s_ref, y_ref, column_ref, part_ref, slots):
     levels, rows, width = s_ref.shape[2:]
     edge, _ = edge_lane(width)
+    base = block_lane()
     lane = iota((rows, width), 1)
     sums = None
     for level in range(levels):
@@ -116,7 +120,7 @@
         y = [[y_ref[i, p, level] for p in range(3)] for i in range(PAIRS)]
         column = jnp.zeros((rows, width), jnp.float32)
         for k, value in enumerate(sum(s, []) + sum(y, [])):
-            at = HISTORY + k
+            at = base + k
             column = jnp.where(lane == at, pltpu.roll(value, (at + width - edge) % width, 1), column)
         column_ref[level] = column
         sums = added(sums, [dot(s[i], y[j]) for i, j in TRI])
@@ -152,6 +156,7 @@
 ):
     levels, rows, width = fields_ref.shape[1:]
     edge, step = edge_lane(width)
+    base = block_lane()
     sub = iota((rows, width), 0)
     lane = iota((rows, width), 1)
     at = lax.axis_index("gx")
@@ -159,7 +164,7 @@
     has_below = at < lax.axis_size("gx") - 1
     sums = None
     for level in range(levels):
-        column = column_ref[level]
+        column = jnp.zeros((rows, width), jnp.float32)
         smooth = []
         for f in range(FIELDS):
             own = fields_ref[f, level]
@@ -171,52 +176,55 @@
             )
             value = 0.25 * (up + 2.0 * own + down)
             along_ref[f, level] = value
-            moved = pltpu.roll(value, (f + width - edge) % width, 1)
-            column = jnp.where(lane == f, moved, column)
-            moved = pltpu.roll(value, (BESIDE + f + width - edge - step) % width, 1)
-            column = jnp.where(lane == BESIDE + f, moved, column)
+            at = base + f
+            moved = pltpu.roll(value, (at + width - edge) % width, 1)
+            column = jnp.where(lane == at, moved, column)
+            moved = pltpu.roll(value, (at + BESIDE + width - edge - step) % width, 1)
+            column = jnp.where(lane == at + BESIDE, moved, column)
             smooth.append(along_y(value))
-        send_ref[level] = column
+        send_ref[0, level] = column
+        send_ref[1, level] = column_ref[level]
         s = [[s_ref[i, p, level] for p in range(3)] for i in range(PAIRS)]
         y = [[y_ref[i, p, level] for p in range(3)] for i in range(PAIRS)]
         sums = added(sums, later_sums(smooth, s, y))
     inside = lane != edge
     sums = [jnp.where(inside, total, 0.0) for total in sums]
-    send_ref[levels] = cross_ref[...] + packed_sums(sums, slots, FIRST)
-
-
-def edge_kernel(own_ref, other_ref, part_ref, slots):
-    levels, rows, width = own_ref.shape
-    levels -= 1
+    send_ref[0, 0, 0:8] = send_ref[0, 0, 0:8] + cross_ref[...] + packed_sums(sums, slots, FIRST)
+
+
+def edge_kernel(own_ref, other_ref, part_ref, other_column_ref, slots):
+    levels, rows, width = own_ref.shape[1:]
     lane = iota((rows, width), 1)
     sums = None
     for level in range(levels):
-        own, other = own_ref[level], other_ref[level]
-        own_edge = 0.25 * (pltpu.roll(own, width - BESIDE, 1) + 2.0 * own + other)
-        other_edge = 0.25 * (pltpu.roll(other, width - BESIDE, 1) + 2.0 * other + own)
-        fields = jnp.where(lane < HALF, own_edge, pltpu.roll(other_edge, HALF, 1))
-        history = jnp.where(lane < HALF, own, pltpu.roll(other, HALF, 1))
+        fields, history = [own_ref[k, level] + other_ref[k, level] for k in range(2)]
+        across = pltpu.roll(fields, 2 * BLOCK, 1)
+        other_column_ref[level] = across
+        smooth = 0.25 * (pltpu.roll(fields, width - BESIDE, 1) + 2.0 * fields + across)
+        if level == 0:
+            part_ref[...] = fields
 
         def entry(array, k):
             return array if k == 0 else pltpu.roll(array, width - k, 1)
 
-        smooth = [entry(fields, f) for f in range(FIELDS)]
-        vectors = [entry(history, HISTORY + k) for k in range(6 * PAIRS)]
+        smooth = [entry(smooth, f) for f in range(FIELDS)]
+        vectors = [entry(history, k) for k in range(6 * PAIRS)]
         vectors = [vectors[k : k + 3] for k in range(0, 6 * PAIRS, 3)]
         sums = added(sums, later_sums(smooth, vectors[:PAIRS], vectors[PAIRS:]))
-    cells = jnp.logical_or(lane == 0, lane == HALF)
+    cells = lane % BLOCK == 0
     sums = [jnp.where(cells, total, 0.0) for total in sums]
-    part_ref[...] = own_ref[levels] + other_ref[levels] + packed_sums(sums, slots, FIRST)
+    part_ref[0:8] = part_ref[0:8] + packed_sums(sums, slots, FIRST)
 
 
 def cells_kernel(along_ref, other_ref, cells_ref):
     levels, rows, width = along_ref.shape[1:]
     edge, _ = edge_lane(width)
+    base = block_lane()
     lane = iota((rows, width), 1)
     for level in range(levels):
         smooth = []
         for f in range(FIELDS):
-            moved = pltpu.roll(other_ref[level], (edge + width - f) % width, 1)
+            moved = pltpu.roll(other_ref[level], (edge + 2 * width - base - f) % width, 1)
             smooth.append(along_y(along_ref[f, level], jnp.where(lane == edge, moved, 0.0)))
         for k, value in enumerate(smooth[0:3] + inverse(smooth[3:9])):
             cells_ref[k, level] = value
@@ -229,7 +237,7 @@
     for part in parts[1:]:
         packed = packed + part[...]
     for g in range(GROUPS):
-        spread_ref[g * 8 : (g + 1) * 8] = jnp.broadcast_to(packed[:, g : g + 1], (8, width))
+        spread_ref[g * 8 : (g + 1) * 8] = jnp.broadcast_to(packed[0:8, SUMS + g : SUMS + g + 1], (8, width))
 
     def entry(k, group=0):
         return spread_ref[8 * group + k : 8 * group + k + 1]
@@ -286,6 +294,10 @@
     return lax.ppermute(x, AXES, pairs)
 
 
+def far_first(n):
+    return range(n - 1, 0, -1)
+
+
 def shot_blocks(partials):
     n = lax.axis_size("shot")
     levels = partials.shape[1] // n
@@ -296,14 +308,19 @@
 
     mine = [block(k) for k in range(n)]
     blocks = [mine[0]]
-    for k in SORDER:
+    for k in far_first(n):
         blocks.append(flipped(mine[k], {"shot": k}))
     return blocks
 
 
+def stages(sizes):
+    n_shot, n_x = sizes
+    return [[{"gx": m | 1} for m in range(2, n_x, 2)], [{"shot": k, "gx": 1} for k in far_first(n_shot)]]
+
+
 def all_sums(part):
     pieces = [part]
-    for stage in STAGES:
+    for stage in stages([lax.axis_size(a) for a in AXES[:2]]):
         part = functools.reduce(jnp.add, pieces)
         pieces = [part]
         for flip in stage:
@@ -327,17 +344,23 @@
     fields, first, last = call(
         functools.partial(sum_kernel, scale, len(blocks)), [tile, edge, edge], blocks
     )
+    below = lax.ppermute(first, "gx", [((i + 1) % n_x, i) for i in range(n_x)])
     above = lax.ppermute(last, "gx", [(i, (i + 1) % n_x) for i in range(n_x)])
-    below = lax.ppermute(first, "gx", [((i + 1) % n_x, i) for i in range(n_x)])
     along, send = call(
         main_kernel,
-        [tile, (levels + 1, rows, width)],
+        [tile, (2, levels, rows, width)],
         [fields, above, below, hist_s, hist_y, column, cross],
         [(8 * LATER * rows, width)],
     )
-    other = flipped(send, {"gy": 1})
-    (part,) = call(edge_kernel, [(rows, width)], [send, other], [(8 * LATER * rows, width)])
-    (cells,) = call(cells_kernel, [tile], [along, other])
+    send = send + flipped(send, {"gx": 1, "gy": 1})
+    other = flipped(send, {"gx": 1})
+    part, other_column = call(
+        edge_kernel,
+        [(rows, width), (levels, rows, width)],
+        [send, other],
+        [(8 * LATER * rows, width)],
+    )
+    (cells,) = call(cells_kernel, [tile], [along, other_column])
     pieces = all_sums(part)
     (direction,) = call(
         functools.partial(combine_kernel, len(pieces)),
@@ -460,15 +483,21 @@
     return combine_terms(cross_gram, curv_gram, hist_dot, pre_dot, solved, hist_s)
 
 
-def per_device(*args):
-    return exchanged(*args)
+def mesh_fits(sizes):
+    n_shot, n_x, n_y = sizes
+    twos = n_shot & (n_shot - 1) == 0 and n_x & (n_x - 1) == 0
+    return twos and n_shot <= 8 and n_x in (2, 4, 8) and n_y == 2
+
+
+def per_device(partials, hist_s, hist_y):
+    rows, width = hist_s.shape[3:]
+    fits = mesh_fits([lax.axis_size(a) for a in AXES]) and rows == 8 and width == 4 * BLOCK
+    return (exchanged if fits else plain_device)(partials, hist_s, hist_y)
 
 
 def solution(mesh):
-    sizes = [mesh.shape[a] for a in AXES]
-    fits = sizes[0] == 4 and sizes[1] == 4 and sizes[2] == 2
     return jax.shard_map(
-        per_device if fits else plain_device,
+        per_device,
         mesh=mesh,
         in_specs=(
             P("shot", None, None, "gx", "gy"),

time: 29.7 us -> 31.1 us (1.047)
  starting transfers between devices: 13.8 us -> 14.6 us
  waiting for transfers between devices: 13.3 us -> 13.9 us
    ppermute x9, starting transfers between devices: 12 us -> 12.8 us  [flipped(): return lax.ppermute(x, AXES, pairs)]
    ppermute x9, waiting for transfers between devices: 12.1 us -> 12.8 us  [flipped(): return lax.ppermute(x, AXES, pairs)]
where the time goes in v2:
time: 31.1 us; the launch traced here: 30.9 us
  starting transfers between devices  14.6 us (47%)
  waiting for transfers between devices  13.9 us (45%)
  Pallas kernels  1.56 us (5%)
  local copies, waits for them, and re-layouts  0.84 us (3%)
    ppermute x9, waiting for transfers between devices, flipped(): return lax.ppermute(x, AXES, pairs)  12.8 us
    ppermute x9, starting transfers between devices, flipped(): return lax.ppermute(x, AXES, pairs)  12.8 us
    ppermute x1, starting transfers between devices, exchanged(): below = lax.ppermute(first, 'gx', [((i + 1) % n_x, i) for i in range(n_x)])  1.73 us
    pallas_call x6, Pallas kernels, call(): pl.pallas_call(kernel, out_shape=out, in_specs=[VMEM] * len(args), out_sp...  1.56 us
    ppermute x1, waiting for transfers between devices, exchanged(): above = lax.ppermute(last, 'gx', [(i, (i + 1) % n_x) for i in range(n_x)])  1.14 us
    dynamic_slice x1, local copies, waits for them, and re-layouts, block(): return lax.dynamic_slice_in_dim(partials, (me ^ k) * levels, levels, axis=1)  0.83 us
  transfers between devices with their start and end apart: 11, of which 8 were waited for; matrix products, arithmetic and copies ran while one was open for 0% of the time, Pallas kernels for 1%

profile of v2, /device:TPU:0, one launch (start us, length us, event | category | flops | bytes accessed | tf_op | source)
XLA Modules:
  0.0 30.9 jit_solution(9353772861240894706)
XLA Ops:
  0.0 0.8 %dynamic-slice_bitcast_fusion = (f32[9,1,8,128]{3,2,1,0:T(8,128)S(1)}, f32[9,1,8,128]{3,2,1,0:T(8,128)S(1)}, f32[9,1,8,128]{3,2,1,0:T(8,128)S(1)}, f32[9,1,8,128]{3,2,1,0:T(8,128)S(1)}) fusion(f32[1,9,4,8,128]{4,3,2,1,0:T(8,128)} %param.3, s32[]{:T(128)S(6)} %select_n.15, s32[]{:T(128)S(6)} %select_n.13, s32[]{:T(128)S(6)} %select_n.12, s32[]{:T(128)S(6)} %select_n.14), kind=kLoop, calls=%fused_computation | loop fusion | bytes 294928 | tf_op jit(solution)/shard_map/dynamic_slice | solution.py:307
  0.8 5.1 %collective-permute-start = (f32[9,1,8,128]{3,2,1,0:T(8,128)S(1)}, f32[9,1,8,128]{3,2,1,0:T(8,128)S(1)}, u32[]{:S(2)}, u32[]{:S(2)}) collective-permute-start(f32[9,1,8,128]{3,2,1,0:T(8,128)S(1)} %get-tuple-element.24), channel_id=1, source_target_pairs={{0,24},{1,25},{2,26},{3,27},{4,28},{5,29},{6,30},{7,31},{8,16},{9,... | collective-permute-start | bytes 110600 | tf_op jit(solution)/shard_map/ppermute | solution.py:294
  6.0 0.0 collective-permute-start.1
  6.0 0.6 %collective-permute-start.2 = (f32[9,1,8,128]{3,2,1,0:T(8,128)S(1)}, f32[9,1,8,128]{3,2,1,0:T(8,128)S(1)}, u32[]{:S(2)}, u32[]{:S(2)}) collective-permute-start(f32[9,1,8,128]{3,2,1,0:T(8,128)S(1)} %get-tuple-element.23), channel_id=1, source_target_pairs={{0,8},{1,9},{2,10},{3,11},{4,12},{5,13},{6,14},{7,15},{8,0},{9,1},... | collective-permute-start | bytes 110600 | tf_op jit(solution)/shard_map/ppermute | solution.py:294
  6.6 1.3 %collective-permute-done.refs_1_ = f32[9,1,8,128]{3,2,1,0:T(8,128)S(1)} collective-permute-done((f32[9,1,8,128]{3,2,1,0:T(8,128)S(1)}, f32[9,1,8,128]{3,2,1,0:T(8,128)S(1)}, u32[]{:S(2)}, u32[]{:S(2)}) %collective-permute-start) | collective-permute-done | bytes 36896 | tf_op jit(solution)/shard_map/ppermute | solution.py:294
  7.9 2.9 %collective-permute-done.1.refs_2_ = f32[9,1,8,128]{3,2,1,0:T(8,128)S(1)} collective-permute-done((f32[9,1,8,128]{3,2,1,0:T(8,128)S(1)}, f32[9,1,8,128]{3,2,1,0:T(8,128)S(1)}, u32[]{:S(2)}, u32[]{:S(2)}) %collective-permute-start.1) | collective-permute-done | bytes 36896 | tf_op jit(solution)/shard_map/ppermute | solution.py:294
  10.8 0.0 collective-permute-done.2.refs_3_
  10.8 0.0 copy-start
  10.8 0.0 copy-start.1
  10.9 0.1 collective-permute-start.3
  10.9 1.7 %collective-permute-start.4 = (f32[1,9,128]{2,1,0:T(8,128)S(1)}, f32[1,9,128]{2,1,0:T(8,128)S(1)}, u32[]{:S(2)}, u32[]{:S(2)}) collective-permute-start(f32[1,9,128]{2,1,0:T(8,128)S(1)} %get-tuple-element.16), channel_id=1, source_target_pairs={{2,0},{4,2},{6,4},{0,6},{3,1},{5,3},{7,5},{1,7},{10,8},{12,10},{14... | collective-permute-start | bytes 13832 | tf_op jit(solution)/shard_map/ppermute | solution.py:347
  12.7 0.0 copy-done
  12.7 0.0 copy-done.1
  12.7 0.2 shard_map.38
  12.8 1.1 %collective-permute-done.3.above_ref = f32[1,9,128]{2,1,0:T(8,128)S(1)} collective-permute-done((f32[1,9,128]{2,1,0:T(8,128)S(1)}, f32[1,9,128]{2,1,0:T(8,128)S(1)}, u32[]{:S(2)}, u32[]{:S(2)}) %collective-permute-start.3) | collective-permute-done | bytes 4640 | tf_op jit(solution)/shard_map/ppermute | solution.py:348
  14.0 0.0 collective-permute-done.4.below_ref
  14.0 0.2 shard_map.39
  14.3 2.7 %collective-permute-start.5 = (f32[2,1,8,128]{3,2,1,0:T(8,128)S(1)}, f32[2,1,8,128]{3,2,1,0:T(8,128)S(1)}, u32[]{:S(2)}, u32[]{:S(2)}) collective-permute-start(f32[2,1,8,128]{3,2,1,0:T(8,128)S(1)} %get-tuple-element.19), channel_id=1, source_target_pairs={{0,3},{1,2},{2,1},{3,0},{4,7},{5,6},{6,5},{7,4},{8,11},{9,10},{10,... | collective-permute-start | bytes 24584 | tf_op jit(solution)/shard_map/ppermute | solution.py:294
  17.0 1.4 %collective-permute-done.5 = f32[2,1,8,128]{3,2,1,0:T(8,128)S(1)} collective-permute-done((f32[2,1,8,128]{3,2,1,0:T(8,128)S(1)}, f32[2,1,8,128]{3,2,1,0:T(8,128)S(1)}, u32[]{:S(2)}, u32[]{:S(2)}) %collective-permute-start.5) | collective-permute-done | bytes 8224 | tf_op jit(solution)/shard_map/ppermute | solution.py:294
  18.3 0.6 %collective-permute-start.6 = (f32[2,1,8,128]{3,2,1,0:T(8,128)S(1)}, f32[2,1,8,128]{3,2,1,0:T(8,128)S(1)}, u32[]{:S(2)}, u32[]{:S(2)}) collective-permute-start(f32[2,1,8,128]{3,2,1,0:T(8,128)S(1)} %add.22.own_ref), channel_id=1, source_target_pairs={{0,2},{1,3},{2,0},{3,1},{4,6},{5,7},{6,4},{7,5},{8,10},{9,11},{10,... | collective-permute-start | bytes 24584 | tf_op jit(solution)/shard_map/ppermute | solution.py:294
  18.9 0.8 %collective-permute-done.6.other_ref = f32[2,1,8,128]{3,2,1,0:T(8,128)S(1)} collective-permute-done((f32[2,1,8,128]{3,2,1,0:T(8,128)S(1)}, f32[2,1,8,128]{3,2,1,0:T(8,128)S(1)}, u32[]{:S(2)}, u32[]{:S(2)}) %collective-permute-start.6) | collective-permute-done | bytes 8224 | tf_op jit(solution)/shard_map/ppermute | solution.py:294
  19.8 0.3 shard_map.40
  20.0 0.5 %collective-permute-start.7 = (f32[8,128]{1,0:T(8,128)S(1)}, f32[8,128]{1,0:T(8,128)S(1)}, u32[]{:S(2)}, u32[]{:S(2)}) collective-permute-start(f32[8,128]{1,0:T(8,128)S(1)} %get-tuple-element.20), channel_id=1, source_target_pairs={{0,6},{1,7},{2,4},{3,5},{4,2},{5,3},{6,0},{7,1},{8,14},{9,15},{10,... | collective-permute-start | bytes 12296 | tf_op jit(solution)/shard_map/ppermute | solution.py:294
  20.5 2.5 %collective-permute-done.7 = f32[8,128]{1,0:T(8,128)S(1)} collective-permute-done((f32[8,128]{1,0:T(8,128)S(1)}, f32[8,128]{1,0:T(8,128)S(1)}, u32[]{:S(2)}, u32[]{:S(2)}) %collective-permute-start.7) | collective-permute-done | bytes 4128 | tf_op jit(solution)/shard_map/ppermute | solution.py:294
  23.1 0.0 collective-permute-start.10
  23.1 3.2 %collective-permute-start.8 = (f32[8,128]{1,0:T(8,128)S(1)}, f32[8,128]{1,0:T(8,128)S(1)}, u32[]{:S(2)}, u32[]{:S(2)}) collective-permute-start(f32[8,128]{1,0:T(8,128)S(1)} %add.23.refs_0_), channel_id=1, source_target_pairs={{0,26},{1,27},{2,24},{3,25},{4,30},{5,31},{6,28},{7,29},{8,18},{9,... | collective-permute-start | bytes 12296 | tf_op jit(solution)/shard_map/ppermute | solution.py:294
  26.3 0.0 collective-permute-start.9
  26.3 0.1 shard_map.41.refs_4_
  26.4 0.0 collective-permute-done.10.refs_3_
  26.4 1.5 %collective-permute-done.8.refs_1_ = f32[8,128]{1,0:T(8,128)S(1)} collective-permute-done((f32[8,128]{1,0:T(8,128)S(1)}, f32[8,128]{1,0:T(8,128)S(1)}, u32[]{:S(2)}, u32[]{:S(2)}) %collective-permute-start.8) | collective-permute-done | bytes 4128 | tf_op jit(solution)/shard_map/ppermute | solution.py:294
  27.9 2.3 %collective-permute-done.9.refs_2_ = f32[8,128]{1,0:T(8,128)S(1)} collective-permute-done((f32[8,128]{1,0:T(8,128)S(1)}, f32[8,128]{1,0:T(8,128)S(1)}, u32[]{:S(2)}, u32[]{:S(2)}) %collective-permute-start.9) | collective-permute-done | bytes 4128 | tf_op jit(solution)/shard_map/ppermute | solution.py:294
  30.2 0.7 %shard_map.42 = f32[3,1,8,128]{3,2,1,0:T(8,128)} custom-call(f32[8,128]{1,0:T(8,128)S(1)} %add.23.refs_0_, f32[8,128]{1,0:T(8,128)S(1)} %collective-permute-done.8.refs_1_, f32[8,128]{1,0:T(8,128)S(1)} %collective-permute-done.9.refs_2_, f32[8,128]{1,0:T(8,128)S(1)} %collective-permute-done.10.refs_3_, f32[9,1,8,128]{3,2,1,0:T(8,128)S(1)} %shard_map.41.refs_4_, ...), custom_call_target="tpu_custom_call" | custom-call | tf_op jit(solution)/shard_map/pallas_call | solution.py:29
  (3 shorter events, 0.0 us)
Async XLA Ops:
  0.8 7.1 %collective-permute-start = (f32[9,1,8,128]{3,2,1,0:T(8,128)S(1)}, f32[9,1,8,128]{3,2,1,0:T(8,128)S(1)}, u32[]{:S(2)}, u32[]{:S(2)}) collective-permute-start(f32[9,1,8,128]{3,2,1,0:T(8,128)S(1)} %get-tuple-element.24), channel_id=1, source_target_pairs={{0,24},{1,25},{2,26},{3,27},{4,28},{5,29},{6,30},{7,31},{8,16},{9,... | collective-permute-start | bytes 110600 | tf_op jit(solution)/shard_map/ppermute | solution.py:294
  6.0 4.9 %collective-permute-start.1 = (f32[9,1,8,128]{3,2,1,0:T(8,128)S(1)}, f32[9,1,8,128]{3,2,1,0:T(8,128)S(1)}, u32[]{:S(2)}, u32[]{:S(2)}) collective-permute-start(f32[9,1,8,128]{3,2,1,0:T(8,128)S(1)} %get-tuple-element.26), channel_id=1, source_target_pairs={{0,16},{1,17},{2,18},{3,19},{4,20},{5,21},{6,22},{7,23},{8,24},{9,... | collective-permute-start | bytes 110600 | tf_op jit(solution)/shard_map/ppermute | solution.py:294
  6.0 4.9 %collective-permute-start.2 = (f32[9,1,8,128]{3,2,1,0:T(8,128)S(1)}, f32[9,1,8,128]{3,2,1,0:T(8,128)S(1)}, u32[]{:S(2)}, u32[]{:S(2)}) collective-permute-start(f32[9,1,8,128]{3,2,1,0:T(8,128)S(1)} %get-tuple-element.23), channel_id=1, source_target_pairs={{0,8},{1,9},{2,10},{3,11},{4,12},{5,13},{6,14},{7,15},{8,0},{9,1},... | collective-permute-start | bytes 110600 | tf_op jit(solution)/shard_map/ppermute | solution.py:294
  10.8 1.8 %copy-start = (f32[5,3,1,8,128]{4,3,2,1,0:T(8,128)S(1)}, f32[5,3,1,8,128]{4,3,2,1,0:T(8,128)}, u32[]{:S(2)}) copy-start(f32[5,3,1,8,128]{4,3,2,1,0:T(8,128)} %refs_5_.1) | copy-start | bytes 184324
  10.8 1.8 %copy-start.1 = (f32[5,3,1,8,128]{4,3,2,1,0:T(8,128)S(1)}, f32[5,3,1,8,128]{4,3,2,1,0:T(8,128)}, u32[]{:S(2)}) copy-start(f32[5,3,1,8,128]{4,3,2,1,0:T(8,128)} %refs_6_.1) | copy-start | bytes 184324
  10.9 3.1 %collective-permute-start.3 = (f32[1,9,128]{2,1,0:T(8,128)S(1)}, f32[1,9,128]{2,1,0:T(8,128)S(1)}, u32[]{:S(2)}, u32[]{:S(2)}) collective-permute-start(f32[1,9,128]{2,1,0:T(8,128)S(1)} %get-tuple-element.15), channel_id=1, source_target_pairs={{0,2},{2,4},{4,6},{6,0},{1,3},{3,5},{5,7},{7,1},{8,10},{10,12},{12... | collective-permute-start | bytes 13832 | tf_op jit(solution)/shard_map/ppermute | solution.py:348
  10.9 3.1 %collective-permute-start.4 = (f32[1,9,128]{2,1,0:T(8,128)S(1)}, f32[1,9,128]{2,1,0:T(8,128)S(1)}, u32[]{:S(2)}, u32[]{:S(2)}) collective-permute-start(f32[1,9,128]{2,1,0:T(8,128)S(1)} %get-tuple-element.16), channel_id=1, source_target_pairs={{2,0},{4,2},{6,4},{0,6},{3,1},{5,3},{7,5},{1,7},{10,8},{12,10},{14... | collective-permute-start | bytes 13832 | tf_op jit(solution)/shard_map/ppermute | solution.py:347
  14.3 4.1 %collective-permute-start.5 = (f32[2,1,8,128]{3,2,1,0:T(8,128)S(1)}, f32[2,1,8,128]{3,2,1,0:T(8,128)S(1)}, u32[]{:S(2)}, u32[]{:S(2)}) collective-permute-start(f32[2,1,8,128]{3,2,1,0:T(8,128)S(1)} %get-tuple-element.19), channel_id=1, source_target_pairs={{0,3},{1,2},{2,1},{3,0},{4,7},{5,6},{6,5},{7,4},{8,11},{9,10},{10,... | collective-permute-start | bytes 24584 | tf_op jit(solution)/shard_map/ppermute | solution.py:294
  18.3 1.4 %collective-permute-start.6 = (f32[2,1,8,128]{3,2,1,0:T(8,128)S(1)}, f32[2,1,8,128]{3,2,1,0:T(8,128)S(1)}, u32[]{:S(2)}, u32[]{:S(2)}) collective-permute-start(f32[2,1,8,128]{3,2,1,0:T(8,128)S(1)} %add.22.own_ref), channel_id=1, source_target_pairs={{0,2},{1,3},{2,0},{3,1},{4,6},{5,7},{6,4},{7,5},{8,10},{9,11},{10,... | collective-permute-start | bytes 24584 | tf_op jit(solution)/shard_map/ppermute | solution.py:294
  20.0 3.0 %collective-permute-start.7 = (f32[8,128]{1,0:T(8,128)S(1)}, f32[8,128]{1,0:T(8,128)S(1)}, u32[]{:S(2)}, u32[]{:S(2)}) collective-permute-start(f32[8,128]{1,0:T(8,128)S(1)} %get-tuple-element.20), channel_id=1, source_target_pairs={{0,6},{1,7},{2,4},{3,5},{4,2},{5,3},{6,0},{7,1},{8,14},{9,15},{10,... | collective-permute-start | bytes 12296 | tf_op jit(solution)/shard_map/ppermute | solution.py:294
  23.1 3.3 %collective-permute-start.10 = (f32[8,128]{1,0:T(8,128)S(1)}, f32[8,128]{1,0:T(8,128)S(1)}, u32[]{:S(2)}, u32[]{:S(2)}) collective-permute-start(f32[8,128]{1,0:T(8,128)S(1)} %add.23.refs_0_), channel_id=1, source_target_pairs={{0,10},{1,11},{2,8},{3,9},{4,14},{5,15},{6,12},{7,13},{8,2},{9,3},... | collective-permute-start | bytes 12296 | tf_op jit(solution)/shard_map/ppermute | solution.py:294
  23.1 4.8 %collective-permute-start.8 = (f32[8,128]{1,0:T(8,128)S(1)}, f32[8,128]{1,0:T(8,128)S(1)}, u32[]{:S(2)}, u32[]{:S(2)}) collective-permute-start(f32[8,128]{1,0:T(8,128)S(1)} %add.23.refs_0_), channel_id=1, source_target_pairs={{0,26},{1,27},{2,24},{3,25},{4,30},{5,31},{6,28},{7,29},{8,18},{9,... | collective-permute-start | bytes 12296 | tf_op jit(solution)/shard_map/ppermute | solution.py:294
  26.3 3.9 %collective-permute-start.9 = (f32[8,128]{1,0:T(8,128)S(1)}, f32[8,128]{1,0:T(8,128)S(1)}, u32[]{:S(2)}, u32[]{:S(2)}) collective-permute-start(f32[8,128]{1,0:T(8,128)S(1)} %add.23.refs_0_), channel_id=1, source_target_pairs={{0,18},{1,19},{2,16},{3,17},{4,22},{5,23},{6,20},{7,21},{8,26},{9,... | collective-permute-start | bytes 12296 | tf_op jit(solution)/shard_map/ppermute | solution.py:294
